TPU v7x, 128 devices: a whole 4x4x4 slice. The times are simulated.
128 devices in a mesh: ray: 16 (over x, z), tile: 8 (over y, core).
Axes of the slice: x: 4, y: 4, z: 4, core: 2. Of those that a mesh axis runs over, the one named last changes fastest.
Arguments:
- data: float32 [64, 262144], P(None, ('ray', 'tile')), may hold values from -6 to 6
- sensitivity: bfloat16 [4096, 256, 512], P(('ray', 'tile')), may hold values from -0.25 to 0.25
- block_tiles: int32 [128, 8, 4], P(('ray', 'tile')), may hold values from 0 to 47
- block_bundles: int32 [128, 8, 4], P(('ray', 'tile')), may hold values from 0 to 7
Outputs:
- solution: float32 [64, 196608], P(None, 'tile')
- residual: float32 [64, 262144], P(None, ('ray', 'tile'))
Inputs may be any that keep to these rules, and one draw needn't show every extreme that they name: `block_tiles`: position of the block's tile among the 48 tiles of the owner given by the second index. `block_bundles`: the block's ray bundle among the device's 8 bundles.
All inputs are finite; a program needn't handle non-finite values.
Results may differ from a plain program's by a relative error of at most 0.004.
The roundings to bfloat16 on the way count: a program that leaves them out, or rounds other values in their place, can miss the bound.
Values may be sent and summed in bfloat16 or wider, within the bound.
A program may use at most 128 MiB of HBM per device.

v0:
```python
import jax
import jax.numpy as jnp
from jax import lax
from jax.sharding import PartitionSpec as P

RB = 256
CB = 512
ITERS = 2
BUND_DEV = 8
TILE_DEV = 48
eps_norm = 1e-06


def per_device(data, sensitivity, block_tiles, block_bundles):
    columns = data.shape[0]
    bundles = block_bundles.reshape(-1)
    requests = lax.all_to_all(block_tiles, "tile", split_axis=1, concat_axis=1, tiled=True).reshape(
        -1
    )
    bundle_onehot = (bundles[:, None] == jnp.arange(BUND_DEV, dtype=jnp.int32)[None, :]).astype(
        jnp.float32
    )
    owner_onehot = (requests[:, None] == jnp.arange(TILE_DEV, dtype=jnp.int32)[None, :]).astype(
        jnp.bfloat16
    )

    def fetch(field_bf):
        owned = field_bf.reshape(columns, TILE_DEV, CB)
        outgoing = jnp.take(owned, requests, axis=1)
        tiles = lax.all_to_all(outgoing, "tile", split_axis=1, concat_axis=1, tiled=True)
        return tiles

    def forward(field_bf):
        tiles = fetch(field_bf)
        partial_value = jnp.einsum(
            "cnk,nrk->ncr", tiles, sensitivity, preferred_element_type=jnp.float32
        )
        summed = jnp.einsum(
            "ncr,nb->cbr", partial_value, bundle_onehot, precision=lax.Precision.HIGHEST
        )
        return summed.reshape(columns, BUND_DEV * RB)

    def adjoint(rays_bf):
        picked = jnp.take(rays_bf.reshape(columns, BUND_DEV, RB), bundles, axis=1)
        terms = jnp.einsum(
            "cnr,nrk->cnk", picked, sensitivity, preferred_element_type=jnp.float32
        ).astype(jnp.bfloat16)
        arrived = lax.all_to_all(terms, "tile", split_axis=1, concat_axis=1, tiled=True)
        owned = jnp.einsum(
            "cnk,nt->ctk", arrived, owner_onehot, preferred_element_type=jnp.float32
        ).reshape(columns, TILE_DEV * CB)
        total = lax.psum(owned, "ray")
        return total

    def cell_norm(field):
        local = jnp.sum(field * field, axis=1)
        total = lax.psum(local, "tile")
        return jnp.sqrt(total + eps_norm)

    def ray_norm(rays):
        total = lax.psum(jnp.sum(rays * rays, axis=1), ("ray", "tile"))
        return jnp.sqrt(total + eps_norm)

    beta_now = ray_norm(data)
    rays_dir = data / beta_now[:, None]
    model_dir = adjoint(rays_dir.astype(jnp.bfloat16))
    alpha_now = cell_norm(model_dir)
    model_dir = model_dir / alpha_now[:, None]
    search = model_dir
    solution = jnp.zeros_like(model_dir)
    phi_bar = beta_now
    rho_bar = alpha_now
    for step in range(ITERS):
        rounded = model_dir.astype(jnp.bfloat16)
        rays_dir = forward(rounded) - alpha_now[:, None] * rays_dir
        beta_now = ray_norm(rays_dir)
        rays_dir = rays_dir / beta_now[:, None]
        rho_now = jnp.sqrt(rho_bar * rho_bar + beta_now * beta_now)
        cosine = rho_bar / rho_now
        sine_part = beta_now / rho_now
        phi_now = cosine * phi_bar
        phi_bar = sine_part * phi_bar
        solution = solution + (phi_now / rho_now)[:, None] * search
        if step + 1 < ITERS:
            model_dir = adjoint(rays_dir.astype(jnp.bfloat16)) - beta_now[:, None] * model_dir
            alpha_now = cell_norm(model_dir)
            model_dir = model_dir / alpha_now[:, None]
            theta_now = sine_part * alpha_now
            rho_bar = -cosine * alpha_now
            search = model_dir - (theta_now / rho_now)[:, None] * search
    residual = data - forward(solution.astype(jnp.bfloat16))
    return (solution, residual)


def solution(mesh):
    return jax.shard_map(
        per_device,
        mesh=mesh,
        in_specs=(
            P(None, ("ray", "tile")),
            P(("ray", "tile"), None, None),
            P(("ray", "tile"), None, None),
            P(("ray", "tile"), None, None),
        ),
        out_specs=(P(None, "tile"), P(None, ("ray", "tile"))),
        check_vma=False,
    )
```

profile of v0, /device:TPU:1, one launch (start us, length us, event | category | flops | bytes accessed | tf_op | source)
XLA Modules:
  0.0 731.6 jit_solution(17410393598439722855)
XLA Ops:
  8.5 6.0 all-to-all-start
  16.5 67.7 %psum.49 = f32[64]{0:T(128)S(1)} all-reduce(f32[64]{0:T(128)S(1)} %multiply_reduce_fusion.4), channel_id=1, replica_groups=mesh['ray'=16,'tile'=8] {'ray','tile'}, use_global_device_ids=true, to_apply=%region_1.0 | all-reduce | flops 64 | bytes 512 | tf_op jit(solution)/shard_map/psum | solution.py:61
  86.1 6.3 convert_bitcast_fusion.1
  92.4 4.4 all-to-all-start.1
  98.1 25.1 %all-to-all-done.1 = bf16[64,32,512]{2,0,1:T(8,128)(2,1)S(1)} async-done(((bf16[64,32,512]{2,0,1:T(8,128)(2,1)}), bf16[64,32,512]{2,0,1:T(8,128)(2,1)S(1)}, u32[]{:S(2)}, u32[]{:S(2)}) %all-to-all-start.1) | async-done | bytes 2097184 | tf_op jit(solution)/shard_map/all_to_all | solution.py:48
  124.9 6.3 copy.39
  131.3 119.1 %all-reduce.3.cloned.1.call-done = f32[64,24576]{1,0:T(8,128)} async-done(((f32[64,24576]{1,0:T(8,128)}), f32[64,24576]{1,0:T(8,128)}) %all-reduce.3.cloned.1.call-update) | async-done | bytes 6291472 | tf_op jit(solution)/shard_map/psum | solution.py:52
  250.4 3.3 multiply_reduce_fusion.1
  253.7 12.4 %psum.51 = f32[64]{0:T(128)S(1)} all-reduce(f32[64]{0:T(128)S(1)} %multiply_reduce_fusion.1), channel_id=1, replica_groups=mesh['ray'=16,'tile'=8] {'tile'}, use_global_device_ids=true, to_apply=%region_4.6 | all-reduce | flops 64 | bytes 512 | tf_op jit(solution)/shard_map/psum | solution.py:57
  266.1 3.2 fusion.37
  269.8 2.0 gather_fusion.1
  273.7 31.7 %all_to_all.30 = bf16[64,32,512]{2,0,1:T(8,128)(2,1)S(1)} all-to-all(bf16[64,32,512]{2,0,1:T(8,128)(2,1)S(1)} %select_bitcast_fusion.2), channel_id=1, replica_groups=mesh['ray'=16,'tile'=8] {'tile'}, dimensions={1} | all-to-all | bytes 4194304 | tf_op jit(solution)/shard_map/all_to_all | solution.py:30
  305.4 6.0 fusion.41
  311.5 2.0 fusion.6
  313.9 64.5 %psum.52 = f32[64]{0:T(128)S(1)} all-reduce(f32[64]{0:T(128)S(1)} %get-tuple-element.11), channel_id=1, replica_groups=mesh['ray'=16,'tile'=8] {'ray','tile'}, use_global_device_ids=true, to_apply=%region_6.0 | all-reduce | flops 64 | bytes 512 | tf_op jit(solution)/shard_map/psum | solution.py:61
  379.2 5.0 convert_bitcast_fusion
  384.2 30.1 %all_to_all.31 = bf16[64,32,512]{2,0,1:T(8,128)(2,1)S(1)} all-to-all(bf16[64,32,512]{2,0,1:T(8,128)(2,1)S(1)} %convert_bitcast_fusion), channel_id=1, replica_groups=mesh['ray'=16,'tile'=8] {'tile'}, dimensions={1} | all-to-all | bytes 4194304 | tf_op jit(solution)/shard_map/all_to_all | solution.py:48
  416.0 6.3 copy.41
  422.3 118.9 %all-reduce.5.cloned.1.call-done = f32[64,24576]{1,0:T(8,128)} async-done(((f32[64,24576]{1,0:T(8,128)}), f32[64,24576]{1,0:T(8,128)}) %all-reduce.5.cloned.1.call-update) | async-done | bytes 6291472 | tf_op jit(solution)/shard_map/psum | solution.py:52
  541.2 5.8 multiply_reduce_fusion
  547.0 12.4 %psum.54 = f32[64]{0:T(128)S(1)} all-reduce(f32[64]{0:T(128)S(1)} %multiply_reduce_fusion), channel_id=1, replica_groups=mesh['ray'=16,'tile'=8] {'tile'}, use_global_device_ids=true, to_apply=%region_9.12 | all-reduce | flops 64 | bytes 512 | tf_op jit(solution)/shard_map/psum | solution.py:57
  559.4 5.2 fusion.10
  565.1 2.0 gather_fusion.3
  568.9 31.7 %all_to_all.32 = bf16[64,32,512]{2,0,1:T(8,128)(2,1)S(1)} all-to-all(bf16[64,32,512]{2,0,1:T(8,128)(2,1)S(1)} %select_bitcast_fusion.1), channel_id=1, replica_groups=mesh['ray'=16,'tile'=8] {'tile'}, dimensions={1} | all-to-all | bytes 4194304 | tf_op jit(solution)/shard_map/all_to_all | solution.py:30
  600.7 6.0 fusion.42
  606.7 2.0 fusion.2
  609.1 64.8 %psum.55 = f32[64]{0:T(128)S(1)} all-reduce(f32[64]{0:T(128)S(1)} %multiply_reduce_fusion.2), channel_id=1, replica_groups=mesh['ray'=16,'tile'=8] {'ray','tile'}, use_global_device_ids=true, to_apply=%region_11.14 | all-reduce | flops 64 | bytes 512 | tf_op jit(solution)/shard_map/psum | solution.py:61
  673.9 7.4 %fusion.38 = (bf16[64,24576]{1,0:T(8,128)(2,1)S(1)}, f32[64,24576]{1,0:T(8,128)}) fusion(f32[64]{0:T(128)S(1)} %multiply_divide_fusion, f32[64]{0:T(128)S(1)} %add_sqrt_fusion, f32[64,24576]{1,0:T(8,128)} %all-reduce.5.cloned.1.call-done, f32[64]{0:T(128)S(1)} %get-tuple-element.13, f32[64]{0:T(128)S(1)} %get-tuple-element.9, ...), kind=kLoop, calls=%fused_computation.76 | loop fusion | flops 15728640 | bytes 22021632 | tf_op jit(solution)/shard_map/convert_element_type | solution.py:91
  681.7 2.0 gather_fusion.4
  685.6 30.1 %all_to_all.33 = bf16[64,32,512]{2,0,1:T(8,128)(2,1)S(1)} all-to-all(bf16[64,32,512]{2,0,1:T(8,128)(2,1)S(1)} %select_bitcast_fusion), channel_id=1, replica_groups=mesh['ray'=16,'tile'=8] {'tile'}, dimensions={1} | all-to-all | bytes 4194304 | tf_op jit(solution)/shard_map/all_to_all | solution.py:30
  715.7 6.0 fusion.43
  721.8 2.0 fusion
  (52 shorter events, 19.5 us)
Async XLA Ops:
  8.5 83.9 %all-to-all-start = ((s32[1,8,4]{2,0,1:T(1,128)}), s32[1,8,4]{2,0,1:T(1,128)S(1)}, u32[]{:S(2)}, u32[]{:S(2)}) async-start(s32[1,8,4]{2,0,1:T(1,128)} %copy.22), calls=%async_computation | async-start | bytes 8192 | tf_op jit(solution)/shard_map/all_to_all | solution.py:17
  92.4 30.8 %all-to-all-start.1 = ((bf16[64,32,512]{2,0,1:T(8,128)(2,1)}), bf16[64,32,512]{2,0,1:T(8,128)(2,1)S(1)}, u32[]{:S(2)}, u32[]{:S(2)}) async-start(bf16[64,32,512]{2,0,1:T(8,128)(2,1)} %convert_bitcast_fusion.1), calls=%async_computation.1 | async-start | bytes 4194304 | tf_op jit(solution)/shard_map/all_to_all | solution.py:48
  96.8 153.6 %all-reduce.3.cloned.1.call-start = ((), (), s32[]{:S(2)}) async-start(), calls=%async_computation.6 | async-start | bytes 12582912 | tf_op jit(solution)/shard_map/psum | solution.py:52
  131.2 410.0 %all-reduce.5.cloned.1.call-start = ((), (), s32[]{:S(2)}) async-start(), calls=%async_computation.7 | async-start | bytes 12582912 | tf_op jit(solution)/shard_map/psum | solution.py:52
  311.4 2.1 copy-start
  313.9 64.7 %copy-start.2 = (f32[64,2048]{1,0:T(8,128)}, f32[64,2048]{1,0:T(8,128)S(1)}, u32[]{:S(2)}) copy-start(f32[64,2048]{1,0:T(8,128)S(1)} %get-tuple-element.12) | copy-start | bytes 1572868
  606.7 2.1 copy-start.3
  721.7 2.1 copy-start.1
Sparse Core Ops, SparseCore 0:
  131.3 119.0 all-reduce.2
  422.4 118.6 all-reduce.4
where the time goes:
time: 733 us; the launch traced here: 732 us
  blocking collectives  346 us (47%)
  waiting for transfers between devices  263 us (36%)
  matrix products  38.8 us (5%)
  other arithmetic  35 us (5%)
  local copies, waits for them, and re-layouts  24.4 us (3%)
  between operations  14.3 us (2%)
  starting transfers between devices  10.4 us (1%)
    psum x2, waiting for transfers between devices, adjoint(): total = lax.psum(owned, 'ray')  238 us
    psum x3, blocking collectives, ray_norm(): total = lax.psum(jnp.sum(rays * rays, axis=1), ('ray', 'tile'))  197 us
    all_to_all x3, blocking collectives, fetch(): lax.all_to_all(outgoing, 'tile', split_axis=1, concat_axis=1, tiled=True)  93.6 us
    all_to_all x1, blocking collectives, adjoint(): lax.all_to_all(terms, 'tile', split_axis=1, concat_axis=1, tiled=True)  30.1 us
    all_to_all x1, waiting for transfers between devices, adjoint(): lax.all_to_all(terms, 'tile', split_axis=1, concat_axis=1, tiled=True)  25.1 us
    psum x2, blocking collectives, cell_norm(): total = lax.psum(local, 'tile')  24.9 us
    dot_general x3, matrix products, forward(): jnp.einsum('cnk,nrk->ncr', tiles, sensitivity, preferred_element_type=jnp...  18.1 us
    unnamed x15, local copies, waits for them, and re-layouts  15.1 us
  transfers between devices with their start and end apart: 4, of which 3 were waited for; matrix products, arithmetic and copies ran while one was open for 2% of the time, Pallas kernels for 0%

commit v1 on v0

--- a/solution.py
+++ b/solution.py
@@ -27,7 +27,12 @@
     def fetch(field_bf):
         owned = field_bf.reshape(columns, TILE_DEV, CB)
         outgoing = jnp.take(owned, requests, axis=1)
-        tiles = lax.all_to_all(outgoing, "tile", split_axis=1, concat_axis=1, tiled=True)
+        tiles = jnp.concatenate(
+            lax.all_to_all(
+                jnp.stack(jnp.split(outgoing, lax.axis_size("tile"), axis=1)), "tile", 0, 0
+            ),
+            axis=1,
+        )
         return tiles
 
     def forward(field_bf):

time: 733 us -> 732 us (level)
  blocking collectives: 346 us -> 375 us
  waiting for transfers between devices: 263 us -> 238 us
    all_to_all x1 -> x2, blocking collectives: 30.1 us -> 60 us  [adjoint(): lax.all_to_all(terms, 'tile', split_axis=1, concat_axis=1, tiled=True)]
    all_to_all x1 -> x0, waiting for transfers between devices: 25.1 us -> none  [adjoint(): lax.all_to_all(terms, 'tile', split_axis=1, concat_axis=1, tiled=True)]
    unnamed x15 -> x36, local copies, waits for them, and re-layouts: 15.1 us -> 15.5 us
  transfers between devices with their start and end apart: 4 -> 3, of which waited for: 3 -> 2; matrix products, arithmetic and copies ran while one was open for 2% -> 0% of each run, Pallas kernels for 0% -> 0%
where the time goes in v1:
time: 732 us; the launch traced here: 731 us
  blocking collectives  375 us (51%)
  waiting for transfers between devices  238 us (33%)
  matrix products  37.4 us (5%)
  other arithmetic  35 us (5%)
  local copies, waits for them, and re-layouts  24.8 us (3%)
  between operations  14.5 us (2%)
    psum x2, waiting for transfers between devices, adjoint(): total = lax.psum(owned, 'ray')  238 us
    psum x3, blocking collectives, ray_norm(): total = lax.psum(jnp.sum(rays * rays, axis=1), ('ray', 'tile'))  197 us
    all_to_all x3, blocking collectives, fetch(): lax.all_to_all(jnp.stack(jnp.split(outgoing, lax.axis_size('tile'), axis=...  93.6 us
    all_to_all x2, blocking collectives, adjoint(): lax.all_to_all(terms, 'tile', split_axis=1, concat_axis=1, tiled=True)  60 us
    psum x2, blocking collectives, cell_norm(): total = lax.psum(local, 'tile')  24.9 us
    dot_general x3, matrix products, forward(): jnp.einsum('cnk,nrk->ncr', tiles, sensitivity, preferred_element_type=jnp...  18.1 us
    unnamed x36, local copies, waits for them, and re-layouts  15.5 us
  transfers between devices with their start and end apart: 3, of which 2 were waited for; matrix products, arithmetic and copies ran while one was open for 0% of the time, Pallas kernels for 0%

profile of v1, /device:TPU:1, one launch (start us, length us, event | category | flops | bytes accessed | tf_op | source)
XLA Modules:
  0.0 731.4 jit_solution(9402864838073610886)
XLA Ops:
  8.5 6.0 all-to-all-start
  16.5 67.7 %psum.49 = f32[64]{0:T(128)S(1)} all-reduce(f32[64]{0:T(128)S(1)} %multiply_reduce_fusion.4), channel_id=1, replica_groups=mesh['ray'=16,'tile'=8] {'ray','tile'}, use_global_device_ids=true, to_apply=%region_1.0 | all-reduce | flops 64 | bytes 512 | tf_op jit(solution)/shard_map/psum | solution.py:66
  87.4 5.0 convert_bitcast_fusion.1
  92.4 29.9 %all_to_all.30 = bf16[64,32,512]{2,0,1:T(8,128)(2,1)S(1)} all-to-all(bf16[64,32,512]{2,0,1:T(8,128)(2,1)S(1)} %convert_bitcast_fusion.1), channel_id=1, replica_groups=mesh['ray'=16,'tile'=8] {'tile'}, dimensions={1} | all-to-all | bytes 4194304 | tf_op jit(solution)/shard_map/all_to_all | solution.py:53
  124.0 6.3 copy.39
  130.3 119.2 %all-reduce.3.cloned.1.call-done = f32[64,24576]{1,0:T(8,128)} async-done(((f32[64,24576]{1,0:T(8,128)}), f32[64,24576]{1,0:T(8,128)}) %all-reduce.3.cloned.1.call-update) | async-done | bytes 6291472 | tf_op jit(solution)/shard_map/psum | solution.py:57
  249.6 3.3 multiply_reduce_fusion.1
  252.8 12.4 %psum.51 = f32[64]{0:T(128)S(1)} all-reduce(f32[64]{0:T(128)S(1)} %multiply_reduce_fusion.1), channel_id=1, replica_groups=mesh['ray'=16,'tile'=8] {'tile'}, use_global_device_ids=true, to_apply=%region_4.6 | all-reduce | flops 64 | bytes 512 | tf_op jit(solution)/shard_map/psum | solution.py:62
  265.3 3.2 fusion.61
  269.0 2.0 gather_fusion.1
  273.1 31.7 %all_to_all.31 = bf16[8,64,4,512]{3,1,2,0:T(8,128)(2,1)S(1)} all-to-all(bf16[8,64,4,512]{3,1,2,0:T(8,128)(2,1)S(1)} %fusion.35), channel_id=1, replica_groups=mesh['ray'=16,'tile'=8] {'tile'}, dimensions={0} | all-to-all | bytes 4194304 | tf_op jit(solution)/shard_map/all_to_all | solution.py:31
  304.8 6.0 fusion.65
  310.8 2.0 fusion.6
  313.2 64.5 %psum.52 = f32[64]{0:T(128)S(1)} all-reduce(f32[64]{0:T(128)S(1)} %get-tuple-element.11), channel_id=1, replica_groups=mesh['ray'=16,'tile'=8] {'ray','tile'}, use_global_device_ids=true, to_apply=%region_6.0 | all-reduce | flops 64 | bytes 512 | tf_op jit(solution)/shard_map/psum | solution.py:66
  378.6 5.0 convert_bitcast_fusion
  383.6 30.1 %all_to_all.32 = bf16[64,32,512]{2,0,1:T(8,128)(2,1)S(1)} all-to-all(bf16[64,32,512]{2,0,1:T(8,128)(2,1)S(1)} %convert_bitcast_fusion), channel_id=1, replica_groups=mesh['ray'=16,'tile'=8] {'tile'}, dimensions={1} | all-to-all | bytes 4194304 | tf_op jit(solution)/shard_map/all_to_all | solution.py:53
  415.4 6.3 copy.41
  421.7 118.9 %all-reduce.5.cloned.1.call-done = f32[64,24576]{1,0:T(8,128)} async-done(((f32[64,24576]{1,0:T(8,128)}), f32[64,24576]{1,0:T(8,128)}) %all-reduce.5.cloned.1.call-update) | async-done | bytes 6291472 | tf_op jit(solution)/shard_map/psum | solution.py:57
  540.6 5.8 multiply_reduce_fusion
  546.3 12.4 %psum.54 = f32[64]{0:T(128)S(1)} all-reduce(f32[64]{0:T(128)S(1)} %multiply_reduce_fusion), channel_id=1, replica_groups=mesh['ray'=16,'tile'=8] {'tile'}, use_global_device_ids=true, to_apply=%region_9.12 | all-reduce | flops 64 | bytes 512 | tf_op jit(solution)/shard_map/psum | solution.py:62
  558.8 5.2 fusion.10
  564.5 2.0 gather_fusion.3
  566.5 1.8 select_bitcast_fusion.1
  568.5 31.7 %all_to_all.33 = bf16[8,64,4,512]{3,1,2,0:T(8,128)(2,1)S(1)} all-to-all(bf16[8,64,4,512]{3,1,2,0:T(8,128)(2,1)S(1)} %fusion.27), channel_id=1, replica_groups=mesh['ray'=16,'tile'=8] {'tile'}, dimensions={0} | all-to-all | bytes 4194304 | tf_op jit(solution)/shard_map/all_to_all | solution.py:31
  600.3 6.0 fusion.66
  606.3 2.0 fusion.2
  608.7 64.8 %psum.55 = f32[64]{0:T(128)S(1)} all-reduce(f32[64]{0:T(128)S(1)} %multiply_reduce_fusion.2), channel_id=1, replica_groups=mesh['ray'=16,'tile'=8] {'ray','tile'}, use_global_device_ids=true, to_apply=%region_11.14 | all-reduce | flops 64 | bytes 512 | tf_op jit(solution)/shard_map/psum | solution.py:66
  673.5 7.4 %fusion.62 = (bf16[64,24576]{1,0:T(8,128)(2,1)S(1)}, f32[64,24576]{1,0:T(8,128)}) fusion(f32[64]{0:T(128)S(1)} %multiply_divide_fusion, f32[64]{0:T(128)S(1)} %add_sqrt_fusion, f32[64,24576]{1,0:T(8,128)} %all-reduce.5.cloned.1.call-done, f32[64]{0:T(128)S(1)} %get-tuple-element.13, f32[64]{0:T(128)S(1)} %get-tuple-element.9, ...), kind=kLoop, calls=%fused_computation.124 | loop fusion | flops 15728640 | bytes 22021632 | tf_op jit(solution)/shard_map/convert_element_type | solution.py:96
  681.3 2.0 gather_fusion.4
  685.4 30.1 %all_to_all.34 = bf16[8,64,4,512]{3,1,2,0:T(8,128)(2,1)S(1)} all-to-all(bf16[8,64,4,512]{3,1,2,0:T(8,128)(2,1)S(1)} %fusion.19), channel_id=1, replica_groups=mesh['ray'=16,'tile'=8] {'tile'}, dimensions={0} | all-to-all | bytes 4194304 | tf_op jit(solution)/shard_map/all_to_all | solution.py:31
  715.5 6.0 fusion.67
  721.6 2.0 fusion
  (74 shorter events, 18.1 us)
Async XLA Ops:
  8.5 76.9 %all-to-all-start = ((s32[1,8,4]{2,0,1:T(1,128)}), s32[1,8,4]{2,0,1:T(1,128)S(1)}, u32[]{:S(2)}, u32[]{:S(2)}) async-start(s32[1,8,4]{2,0,1:T(1,128)} %copy.22), calls=%async_computation | async-start | bytes 8192 | tf_op jit(solution)/shard_map/all_to_all | solution.py:17
  14.5 235.1 %all-reduce.3.cloned.1.call-start = ((), (), s32[]{:S(2)}) async-start(), calls=%async_computation.6 | async-start | bytes 12582912 | tf_op jit(solution)/shard_map/psum | solution.py:57
  130.3 410.3 %all-reduce.5.cloned.1.call-start = ((), (), s32[]{:S(2)}) async-start(), calls=%async_computation.7 | async-start | bytes 12582912 | tf_op jit(solution)/shard_map/psum | solution.py:57
  310.8 2.1 copy-start
  313.2 64.7 %copy-start.2 = (f32[64,2048]{1,0:T(8,128)}, f32[64,2048]{1,0:T(8,128)S(1)}, u32[]{:S(2)}) copy-start(f32[64,2048]{1,0:T(8,128)S(1)} %get-tuple-element.12) | copy-start | bytes 1572868
  606.3 2.1 copy-start.3
  721.6 2.1 copy-start.1
Sparse Core Ops, SparseCore 0:
  130.4 119.1 all-reduce.2
  421.8 118.6 all-reduce.4
